TPU v7x, 32 devices: a whole 2x2x4 slice. The times are simulated.
32 devices in a mesh: fsdp: 8 (over z, y), tp: 4 (over x, core).
Axes of the slice: x: 2, y: 2, z: 4, core: 2. Of those that a mesh axis runs over, the one named last changes fastest.
Arguments:
- layer_input: bfloat16 [8192, 768], P(('fsdp', 'tp')), may hold values from -12 to 12
- out_cotangent: bfloat16 [8192, 768], P(('fsdp', 'tp')), may hold values from -12 to 12
- segments: int32 [8, 1024], P('fsdp'), may hold values from 0 to 3, never falling along the last dimension, each value on 1 to 512 neighbouring positions
- norm_gain: float32 [768], replicated, may hold values from 0.5 to 1.5
- norm_bias: float32 [768], replicated, may hold values from -3 to 3
- qkv_weight: bfloat16 [768, 2304], P('fsdp', 'tp'), may hold values from -20 to 20
- qkv_bias: float32 [2304], P('tp'), may hold values from -3 to 3
- out_weight: bfloat16 [768, 768], P('tp', 'fsdp'), may hold values from -0.875 to 0.875
- out_bias: float32 [768], replicated, may hold values from -3 to 3
- up_weight: bfloat16 [768, 3072], P('fsdp', 'tp'), may hold values from -0.21875 to 0.21875
- up_bias: float32 [3072], P('tp'), may hold values from -3 to 3
- down_weight: bfloat16 [3072, 768], P('tp', 'fsdp'), may hold values from -0.109375 to 0.109375
- down_bias: float32 [768], replicated, may hold values from -3 to 3
Outputs:
- layer_output: bfloat16 [8192, 768], P(('fsdp', 'tp'))
- input_grad: bfloat16 [8192, 768], P(('fsdp', 'tp'))
- norm_gain_grad: float32 [768], replicated
- norm_bias_grad: float32 [768], replicated
- qkv_weight_grad: float32 [768, 2304], P('fsdp', 'tp')
- qkv_bias_grad: float32 [2304], P('tp')
- out_weight_grad: float32 [768, 768], P('tp', 'fsdp')
- out_bias_grad: float32 [768], replicated
- up_weight_grad: float32 [768, 3072], P('fsdp', 'tp')
- up_bias_grad: float32 [3072], P('tp')
- down_weight_grad: float32 [3072, 768], P('tp', 'fsdp')
- down_bias_grad: float32 [768], replicated
Inputs may be any that keep to these rules, and one draw needn't show every extreme that they name: `segments`: each row is one sequence of 1024 tokens; its numbers name documents, never fall along the row, and each document spans 1 to 512 tokens, one exactly 512.
All inputs are finite; a program needn't handle non-finite values.
Results may differ from a plain program's by a relative error of at most 0.01.
Values may be sent and summed in bfloat16 or wider, within the bound.
A program may use at most 128 MiB of HBM per device.

v0:
```python
import functools

import jax
import jax.numpy as jnp
from jax import lax
from jax.experimental import pallas as pl
from jax.experimental.pallas import tpu as pltpu
from jax.sharding import PartitionSpec as P

HEAD_DIM = 64
ROT = 16


EPSILON = 1e-05
ROTARY_BASE = 10000.0


def layer_norm(values, gain, shift):
    center = values - jnp.mean(values, axis=-1, keepdims=True)
    spread = jnp.mean(center * center, axis=-1, keepdims=True)
    inverse = lax.rsqrt(spread + EPSILON)
    normed = center * inverse
    return (normed, inverse, normed * gain + shift)


def gelu_value(pre_act):
    return 0.5 * pre_act * (1.0 + lax.erf(pre_act * 0.7071067811865476))


def gelu_slope(pre_act):
    return (
        0.5 * (1.0 + lax.erf(pre_act * 0.7071067811865476))
        + pre_act * jnp.exp(-0.5 * pre_act * pre_act) * 0.3989422804014327
    )


def positions_of(segment_row):
    length = segment_row.shape[0]
    counter = jnp.arange(length, dtype=jnp.int32)
    is_start = jnp.concatenate(
        [jnp.ones((1,), dtype=jnp.bool_), segment_row[1:] != segment_row[:-1]]
    )
    starts = lax.cummax(jnp.where(is_start, counter, jnp.zeros_like(counter)), axis=0)
    return counter - starts


def rotary_tables(positions):
    halves = ROT // 2
    inverse_freq = ROTARY_BASE ** (-(jnp.arange(halves, dtype=jnp.float32) * 2.0) / ROT)
    angles = positions.astype(jnp.float32)[:, None] * inverse_freq[None, :]
    cos_table = jnp.cos(angles)
    sin_table = jnp.sin(angles)
    return (
        jnp.concatenate([cos_table, cos_table], axis=-1),
        jnp.concatenate([sin_table, sin_table], axis=-1),
    )


def cross_rows(left, right):
    return lax.dot_general(
        left, right, (((0,), (0,)), ((), ())), preferred_element_type=jnp.float32
    )


def cross_cols(left, right):
    return lax.dot_general(
        left, right, (((1,), (1,)), ((), ())), preferred_element_type=jnp.float32
    )


MESH = pl.DeviceIdType.MESH


def place(fsdp, tp):
    f = lax.axis_index("fsdp")
    t = lax.axis_index("tp")
    pair = lax.rem(f, 2)
    line = lax.div(f, 2)
    return f, t, pair, line


def remote(source, target, send, recv, device):
    return pltpu.make_async_remote_copy(
        src_ref=source,
        dst_ref=target,
        send_sem=send,
        recv_sem=recv,
        device_id=device,
        device_id_type=MESH,
    )


def each(first, last, action):
    def step_of(step, carry):
        action(step)
        return carry

    lax.fori_loop(first, last, step_of, 0)


def greet(fsdp, tp):
    f, t, _, _ = place(fsdp, tp)
    barrier = pltpu.get_barrier_semaphore()
    each(
        1,
        fsdp,
        lambda step: pl.semaphore_signal(
            barrier, inc=1, device_id=(lax.rem(f + step, fsdp), t), device_id_type=MESH
        ),
    )
    each(
        1,
        tp,
        lambda step: pl.semaphore_signal(
            barrier, inc=1, device_id=(f, lax.rem(t + step, tp)), device_id_type=MESH
        ),
    )
    pl.semaphore_wait(barrier, fsdp + tp - 2)


def gather_kernel(
    fsdp, tp, w_ref, h_ref, c_ref, w_out, h_out, c_out, w_send, w_recv, p_send, p_recv, r_send, r_recv
):
    f, t, pair, line = place(fsdp, tp)
    lines = fsdp // 2
    greet(fsdp, tp)
    partner = 2 * line + 1 - pair

    def along(step, slot):
        other = lax.rem(line + step, lines)
        return remote(
            w_ref, w_out.at[slot], w_send.at[step], w_recv.at[step], (2 * other + pair, t)
        )

    def across(step, source, slot):
        return remote(source, w_out.at[slot], p_send.at[step], p_recv.at[step], (partner, t))

    def beside(step, which, source, target, slot):
        return remote(
            source,
            target.at[slot],
            r_send.at[which, step],
            r_recv.at[which, step],
            (f, lax.rem(t + step, tp)),
        )

    def came(step, side):
        return 2 * lax.rem(line + lines - step, lines) + side

    across(0, w_ref, f).start()
    each(1, lines, lambda step: along(step, f).start())
    each(1, tp, lambda step: beside(step, 0, h_ref, h_out, t).start())
    each(1, tp, lambda step: beside(step, 1, c_ref, c_out, t).start())
    w_out[f] = w_ref[...]
    h_out[t] = h_ref[...]
    c_out[t] = c_ref[...]

    def forward(step):
        slot = came(step, pair)
        along(step, slot).wait_recv()
        across(step, w_out.at[slot], slot).start()

    each(1, lines, forward)

    def settle(step):
        slot = lax.rem(t + tp - step, tp)
        beside(step, 0, h_ref, h_out, slot).wait()
        beside(step, 1, c_ref, c_out, slot).wait()

    each(1, tp, settle)
    each(1, lines, lambda step: along(step, f).wait_send())

    def finish(step):
        across(step, w_ref, came(step, 1 - pair)).wait()

    each(0, lines, finish)


def gather_all(weights, features, cotangent):
    fsdp = lax.axis_size("fsdp")
    tp = lax.axis_size("tp")
    vmem = pl.BlockSpec(memory_space=pltpu.VMEM)
    shapes = (
        jax.ShapeDtypeStruct((fsdp,) + weights.shape, weights.dtype),
        jax.ShapeDtypeStruct((tp,) + features.shape, features.dtype),
        jax.ShapeDtypeStruct((tp,) + cotangent.shape, cotangent.dtype),
    )
    dma = pltpu.SemaphoreType.DMA
    w_all, h_all, c_all = pl.pallas_call(
        functools.partial(gather_kernel, fsdp, tp),
        out_shape=shapes,
        in_specs=[vmem] * 3,
        out_specs=(vmem,) * 3,
        scratch_shapes=[
            dma((fsdp // 2,)),
            dma((fsdp // 2,)),
            dma((fsdp // 2,)),
            dma((fsdp // 2,)),
            dma((2, tp)),
            dma((2, tp)),
        ],
        compiler_params=pltpu.CompilerParams(
            collective_id=1, has_side_effects=True, vmem_limit_bytes=48 * 1024 * 1024
        ),
        name="gather_all",
    )(weights, features, cotangent)
    return (
        w_all.reshape(fsdp * weights.shape[0], weights.shape[1]),
        h_all.reshape(tp * features.shape[0], features.shape[1]),
        c_all.reshape(tp * cotangent.shape[0], cotangent.shape[1]),
    )


def scatter_kernel(
    fsdp,
    tp,
    many,
    *refs,
):
    g_refs, refs = refs[:many], refs[many:]
    b_ref, d_ref, n_ref, v_ref = refs[:4]
    g_outs, refs = refs[4 : 4 + many], refs[4 + many :]
    b_out, d_out, v_out = refs[:3]
    halves, joined, lands = (refs[3 + many * i : 3 + many * (i + 1)] for i in range(3))
    (
        b_land,
        d_land,
        rows,
        first,
        second,
        p_send,
        p_recv,
        w_send,
        w_recv,
        r_send,
        r_recv,
        v_send,
        v_recv,
        u_send,
        u_recv,
    ) = refs[3 + 3 * many :]
    f, t, pair, line = place(fsdp, tp)
    lines = fsdp // 2
    greet(fsdp, tp)
    partner = 2 * line + 1 - pair

    def ahead(step):
        return lax.rem(line + step, lines)

    def across(i, step):
        return remote(
            g_refs[i].at[2 * ahead(step) + 1 - pair],
            halves[i].at[step],
            p_send.at[i, step],
            p_recv.at[i, step],
            (partner, t),
        )

    def along(i, step):
        return remote(
            joined[i].at[step],
            lands[i].at[step],
            w_send.at[i, step],
            w_recv.at[i, step],
            (2 * ahead(step) + pair, t),
        )

    def beside(step, which, source, target):
        return remote(
            source.at[lax.rem(t + step, tp)],
            target.at[step],
            r_send.at[which, step],
            r_recv.at[which, step],
            (f, lax.rem(t + step, tp)),
        )

    def start_beside(step):
        beside(step, 1, d_ref, d_land).start()
        beside(step, 0, b_ref, b_land).start()

    def start_across(step):
        for i in range(many):
            across(i, step).start()

    each(1, lines, start_across)
    start_across(0)
    each(1, tp, start_beside)

    def join(step):
        for i in range(many):
            across(i, step).wait_recv()
            joined[i][step] = (
                g_refs[i][2 * ahead(step) + pair].astype(jnp.float32)
                + halves[i][step].astype(jnp.float32)
            ).astype(joined[i].dtype)
            along(i, step).start()

    each(1, lines, join)
    for i in range(many):
        across(i, 0).wait_recv()
        g_outs[i][...] = g_refs[i][f].astype(jnp.float32) + halves[i][0].astype(jnp.float32)

    d_out[...] = d_ref[t].astype(jnp.float32)
    b_out[...] = b_ref[t].astype(jnp.float32)

    def gather_d(step):
        beside(step, 1, d_ref, d_land).wait()
        d_out[...] += d_land[step].astype(jnp.float32)

    def gather_b(step):
        beside(step, 0, b_ref, b_land).wait()
        b_out[...] += b_land[step].astype(jnp.float32)

    each(1, tp, gather_d)
    rows[...] = v_ref[...]
    rows[0:1] = jnp.sum(d_out[...] * n_ref[...], axis=0, keepdims=True)
    rows[1:2] = jnp.sum(d_out[...], axis=0, keepdims=True)

    def spread(step, slot):
        return remote(
            rows,
            first.at[slot],
            v_send.at[step],
            v_recv.at[step],
            (lax.rem(f + step, fsdp), t),
        )

    each(1, fsdp, lambda step: spread(step, f).start())
    first[f] = rows[...]
    each(1, tp, gather_b)

    def collect(step):
        for i in range(many):
            along(i, step).wait_recv()
            g_outs[i][...] += lands[i][step].astype(jnp.float32)

    each(1, lines, collect)
    each(1, fsdp, lambda step: spread(step, lax.rem(f + fsdp - step, fsdp)).wait())
    total = lax.fori_loop(1, fsdp, lambda step, value: value + first[step], first[0])
    second[t] = total[:8]
    v_out[...] = total

    def share(step, slot):
        return remote(
            second.at[t],
            second.at[slot],
            u_send.at[step],
            u_recv.at[step],
            (f, lax.rem(t + step, tp)),
        )

    each(1, tp, lambda step: share(step, t).start())

    def sent_along(step):
        for i in range(many):
            along(i, step).wait_send()

    def sent_across(step):
        for i in range(many):
            across(i, step).wait_send()

    each(1, lines, sent_along)
    each(0, lines, sent_across)
    each(1, tp, lambda step: share(step, lax.rem(t + tp - step, tp)).wait())
    whole = second[0]
    for step in range(1, tp):
        whole = whole + second[step]
    v_out[:8] = whole


def scatter_all(grads, branch, feature_grad, normed, vectors):
    fsdp = lax.axis_size("fsdp")
    tp = lax.axis_size("tp")
    lines = fsdp // 2
    grads = [grad.reshape(fsdp, -1, grad.shape[1]) for grad in grads]
    many = len(grads)
    branch = branch.reshape(tp, -1, branch.shape[1])
    feature_grad = feature_grad.reshape(tp, -1, feature_grad.shape[1])
    vmem = pl.BlockSpec(memory_space=pltpu.VMEM)
    dma = pltpu.SemaphoreType.DMA
    f32 = jnp.float32
    return pl.pallas_call(
        functools.partial(scatter_kernel, fsdp, tp, many),
        out_shape=(
            *(jax.ShapeDtypeStruct(grad.shape[1:], f32) for grad in grads),
            jax.ShapeDtypeStruct(branch.shape[1:], f32),
            jax.ShapeDtypeStruct(feature_grad.shape[1:], f32),
            jax.ShapeDtypeStruct(vectors.shape, f32),
        ),
        in_specs=[vmem] * (many + 4),
        out_specs=(vmem,) * (many + 3),
        scratch_shapes=[
            *(
                pltpu.VMEM((lines,) + grad.shape[1:], grad.dtype)
                for _ in range(3)
                for grad in grads
            ),
            pltpu.VMEM(branch.shape, branch.dtype),
            pltpu.VMEM(feature_grad.shape, feature_grad.dtype),
            pltpu.VMEM(vectors.shape, f32),
            pltpu.VMEM((fsdp,) + vectors.shape, f32),
            pltpu.VMEM((tp, 8, vectors.shape[1]), f32),
            dma((many, lines)),
            dma((many, lines)),
            dma((many, lines)),
            dma((many, lines)),
            dma((2, tp)),
            dma((2, tp)),
            dma((fsdp,)),
            dma((fsdp,)),
            dma((tp,)),
            dma((tp,)),
        ],
        compiler_params=pltpu.CompilerParams(
            collective_id=2, has_side_effects=True, vmem_limit_bytes=56 * 1024 * 1024
        ),
        name="scatter_all",
    )(*grads, branch, feature_grad, normed, vectors)


MOST = 512
SPAN = 256


def attention_kernel(
    heads,
    f_ref,
    c_ref,
    wq_ref,
    bq_ref,
    wo_ref,
    cos_ref,
    sin_ref,
    turn_ref,
    col_ref,
    row_ref,
    o_ref,
    dx_ref,
    sum_ref,
    queries,
    keys_in,
    values_in,
    grads_in,
    mixed,
    grad_q,
    grad_k,
    grad_v,
    x_ref,
    do_ref,
):
    length = f_ref.shape[0]
    span = min(SPAN, length)
    scale = HEAD_DIM ** (-0.5)
    two = 2 * HEAD_DIM
    f32 = jnp.float32
    bf16 = jnp.bfloat16

    def turned(value, axis):
        return lax.dot_general(
            value,
            turn_ref[...],
            (((1,), (axis,)), ((), ())),
            precision=lax.Precision.HIGHEST,
            preferred_element_type=f32,
        )

    for first in range(0, length, span):
        part = slice(first, first + span)
        x_ref[part] = (
            jnp.dot(f_ref[part], wq_ref[...], preferred_element_type=f32) + bq_ref[...]
        )
        do_ref[part] = jnp.dot(c_ref[part], wo_ref[...], preferred_element_type=f32).astype(bf16)
    for n in range(heads):
        base = 3 * HEAD_DIM * n
        for first in range(0, length, span):
            part = slice(first, first + span)
            both = x_ref[part, base : base + two]
            both = both * cos_ref[part] + turned(both, 0) * sin_ref[part]
            queries[n, part] = both[:, :HEAD_DIM].astype(bf16) * bf16(scale)
            keys_in[n, part] = both[:, HEAD_DIM:].astype(bf16)
            values_in[n, part] = x_ref[part, base + two : base + two + HEAD_DIM].astype(bf16)
            grads_in[n, part] = do_ref[part, n * HEAD_DIM : (n + 1) * HEAD_DIM]
    grad_k[...] = jnp.zeros_like(grad_k)
    grad_v[...] = jnp.zeros_like(grad_v)

    def one_head(n, carry):
        for first in range(0, length, span):
            last = first + span
            low = max(0, (first - MOST) // span * span)
            part = slice(first, last)
            window = slice(low, last)
            q = queries[n, part]
            k = keys_in[n, window]
            v = values_in[n, window]
            g = grads_in[n, part]
            shape = (span, last - low)
            allowed = (col_ref[part] == row_ref[:, window]) & (
                lax.broadcasted_iota(jnp.int32, shape, 0) + first
                >= lax.broadcasted_iota(jnp.int32, shape, 1) + low
            )
            scores = jnp.where(allowed, cross_cols(q, k), -1e30)
            exps = jnp.exp(scores - jnp.max(scores, axis=-1, keepdims=True))
            probs = exps * (1.0 / jnp.sum(exps, axis=-1, keepdims=True))
            weights = probs.astype(bf16)
            out = jnp.dot(weights, v, preferred_element_type=f32).astype(bf16)
            mixed[n, part] = out
            delta = jnp.sum(g.astype(f32) * out.astype(f32), axis=-1, keepdims=True)
            grad_probs = cross_cols(g, v)
            grad_scores = (probs * (grad_probs - delta)).astype(bf16)
            grad_q[n, part] = jnp.dot(grad_scores, k, preferred_element_type=f32) * scale
            grad_k[n, window] += cross_rows(grad_scores, q)
            grad_v[n, window] += cross_rows(weights, g)
        return carry

    lax.fori_loop(0, heads, one_head, 0)

    sum_ref[...] = jnp.zeros_like(sum_ref)
    for first in range(0, length, span):
        part = slice(first, first + span)
        pieces = []
        for n in range(heads):
            both = jnp.concatenate([grad_q[n, part], grad_k[n, part]], axis=1)
            both = both * cos_ref[part] + turned(both * sin_ref[part], 1)
            pieces += [both, grad_v[n, part]]
        whole = jnp.concatenate(pieces, axis=1)
        sum_ref[...] += jnp.sum(whole, axis=0, keepdims=True)
        dx_ref[part] = whole.astype(bf16)
        o_ref[part] = jnp.concatenate([mixed[n, part] for n in range(heads)], axis=1)


def attention_branch(features, grad_rows, qkv_full, qkv_bias, out_full, segment_row):
    length = features.shape[0]
    heads = qkv_full.shape[1] // (3 * HEAD_DIM)
    cos_table, sin_table = rotary_tables(positions_of(segment_row))
    rest = ((0, 0), (0, HEAD_DIM - ROT))
    cos_full = jnp.tile(jnp.pad(cos_table, rest, constant_values=1.0), (1, 2))
    sin_full = jnp.tile(jnp.pad(sin_table, rest), (1, 2))
    half = ROT // 2
    source = jnp.arange(2 * HEAD_DIM)[:, None]
    target = jnp.arange(2 * HEAD_DIM)[None, :]
    inner = target % HEAD_DIM
    turn = jnp.where(
        (inner < half) & (source == target + half),
        -1.0,
        jnp.where((inner >= half) & (inner < ROT) & (source == target - half), 1.0, 0.0),
    ).astype(jnp.float32)
    wide = qkv_full.shape[1]
    vmem = pl.BlockSpec(memory_space=pltpu.VMEM)
    mixed_rows, packed_grad, sums = pl.pallas_call(
        functools.partial(attention_kernel, heads),
        out_shape=(
            jax.ShapeDtypeStruct((length, heads * HEAD_DIM), jnp.bfloat16),
            jax.ShapeDtypeStruct((length, wide), jnp.bfloat16),
            jax.ShapeDtypeStruct((1, wide), jnp.float32),
        ),
        in_specs=[vmem] * 10,
        out_specs=(vmem,) * 3,
        scratch_shapes=[pltpu.VMEM((heads, length, HEAD_DIM), jnp.bfloat16)] * 5
        + [pltpu.VMEM((heads, length, HEAD_DIM), jnp.float32)] * 3
        + [
            pltpu.VMEM((length, wide), jnp.float32),
            pltpu.VMEM((length, heads * HEAD_DIM), jnp.bfloat16),
        ],
        compiler_params=pltpu.CompilerParams(vmem_limit_bytes=56 * 1024 * 1024),
        name="attention",
    )(
        features,
        grad_rows,
        qkv_full,
        qkv_bias[None],
        out_full,
        cos_full,
        sin_full,
        turn,
        segment_row[:, None],
        segment_row[None, :],
    )
    return mixed_rows, packed_grad, sums[0]


def body(
    layer_input,
    out_cotangent,
    segments,
    norm_gain,
    norm_bias,
    qkv_weight,
    qkv_bias,
    out_weight,
    out_bias,
    up_weight,
    up_bias,
    down_weight,
    down_bias,
):
    width_qkv = qkv_weight.shape[1]
    width_out = out_weight.shape[0]
    width_up = up_weight.shape[1]
    own_rows = layer_input.astype(jnp.float32)
    normed, inverse, shifted = layer_norm(own_rows, norm_gain, norm_bias)
    w_all, features, grad_rows = gather_all(
        jnp.concatenate([up_weight, down_weight.T, qkv_weight, out_weight.T], axis=1),
        shifted.astype(jnp.bfloat16),
        out_cotangent,
    )
    ends = (width_up, 2 * width_up, 2 * width_up + width_qkv)
    full_up, full_down, full_qkv, full_out = jnp.split(w_all, ends, axis=1)

    pre_act = jnp.dot(features, full_up, preferred_element_type=jnp.float32) + up_bias
    gelu_rows = gelu_value(pre_act).astype(jnp.bfloat16)
    grad_pre = jnp.dot(grad_rows, full_down, preferred_element_type=jnp.float32) * gelu_slope(
        pre_act
    )
    pre_grads = grad_pre.astype(jnp.bfloat16)
    up_bias_part = jnp.sum(grad_pre, axis=0)
    mixed_rows, packed_bf, qkv_bias_part = attention_branch(
        features, grad_rows, full_qkv, qkv_bias, full_out, segments[0]
    )
    branch = cross_cols(mixed_rows, full_out) + cross_cols(gelu_rows, full_down)
    feature_grad = cross_cols(packed_bf, full_qkv) + cross_cols(pre_grads, full_up)
    grads = [
        cross_rows(features, pre_grads).astype(jnp.bfloat16),
        cross_rows(grad_rows, gelu_rows).astype(jnp.bfloat16),
        cross_rows(features, packed_bf).astype(jnp.bfloat16),
        cross_rows(grad_rows, mixed_rows).astype(jnp.bfloat16),
    ]
    cot_rows = out_cotangent.astype(jnp.float32)
    model = own_rows.shape[1]
    biases = jnp.concatenate([qkv_bias_part, up_bias_part])
    bias_rows = -(-biases.shape[0] // model)
    biases = jnp.pad(biases, (0, bias_rows * model - biases.shape[0])).reshape(bias_rows, model)
    vectors = jnp.concatenate(
        [
            jnp.zeros((2, model), jnp.float32),
            jnp.sum(cot_rows, axis=0)[None],
            jnp.zeros((5, model), jnp.float32),
            biases,
            jnp.zeros((-bias_rows % 8, model), jnp.float32),
        ]
    )
    up_grad, down_grad, qkv_grad, out_grad, branch, row_grad, sums = scatter_all(
        grads,
        branch.astype(jnp.bfloat16),
        feature_grad.astype(jnp.bfloat16),
        normed,
        vectors,
    )
    layer_output = (own_rows + branch + out_bias + down_bias).astype(jnp.bfloat16)
    gain_grad, shift_grad, bias_grad = sums[0], sums[1], sums[2]
    bias_flat = sums[8 : 8 + bias_rows].reshape(-1)
    qkv_bias_grad = bias_flat[:width_qkv]
    up_bias_grad = bias_flat[width_qkv : width_qkv + width_up]
    scaled = row_grad * norm_gain
    input_grad = (
        cot_rows
        + inverse
        * (
            scaled
            - jnp.mean(scaled, axis=-1, keepdims=True)
            - normed * jnp.mean(scaled * normed, axis=-1, keepdims=True)
        )
    ).astype(jnp.bfloat16)
    return (
        layer_output,
        input_grad,
        gain_grad,
        shift_grad,
        qkv_grad,
        qkv_bias_grad,
        out_grad.T,
        bias_grad,
        up_grad,
        up_bias_grad,
        down_grad.T,
        bias_grad,
    )


def solution(mesh):
    in_specs = (
        P(("fsdp", "tp"), None),
        P(("fsdp", "tp"), None),
        P("fsdp", None),
        P(),
        P(),
        P("fsdp", "tp"),
        P("tp"),
        P("tp", "fsdp"),
        P(),
        P("fsdp", "tp"),
        P("tp"),
        P("tp", "fsdp"),
        P(),
    )
    out_specs = (
        P(("fsdp", "tp"), None),
        P(("fsdp", "tp"), None),
        P(),
        P(),
        P("fsdp", "tp"),
        P("tp"),
        P("tp", "fsdp"),
        P(),
        P("fsdp", "tp"),
        P("tp"),
        P("tp", "fsdp"),
        P(),
    )
    return jax.shard_map(body, mesh=mesh, in_specs=in_specs, out_specs=out_specs, check_vma=False)
```

profile of v0, /device:TPU:0, one launch (start us, length us, event | category | flops | bytes accessed | tf_op | source)
XLA Modules:
  0.0 216.6 jit_solution(13545060506827829868)
XLA Ops:
  1.6 1.1 convert_reduce_fusion
  2.7 1.2 fusion.14
  4.0 1.3 broadcast_in_dim.24.bq_ref
  5.9 1.1 convert_reduce_fusion.1
  7.5 0.9 copy.29
  9.6 1.0 copy.31.sin_ref
  10.6 1.0 copy.30.cos_ref
  11.7 1.0 copy.32.col_ref
  12.7 1.1 fusion.12
  13.8 57.8 %gather_all.1 = (bf16[8,96,2304]{2,1,0:T(8,128)(2,1)}, bf16[4,256,768]{2,1,0:T(8,128)(2,1)S(1)}, bf16[4,256,768]{2,1,0:T(8,128)(2,1)S(1)}) custom-call(bf16[96,2304]{1,0:T(8,128)(2,1)S(1)} %concatenate.20.w_ref, bf16[256,768]{1,0:T(8,128)(2,1)S(1)} %get-tuple-element.68.h_ref, bf16[256,768]{1,0:T(8,128)(2,1)S(1)} %copy-done), custom_call_target="tpu_custom_call" | custom-call | tf_op jit(solution)/shard_map/gather_all/pallas_call | solution.py:189
  71.7 1.2 copy-done.1
  72.8 1.2 copy-done.3
  74.0 1.9 split.19.wo_ref
  75.9 2.3 %split.18.wq_ref = bf16[768,576]{1,0:T(8,128)(2,1)} slice(bf16[768,2304]{1,0:T(8,128)(2,1)} %bitcast.55), slice={[0:768], [1536:2112]} | slice | bytes 1769472 | tf_op jit(solution)/shard_map/split | solution.py:607
  78.3 21.0 %attention.1 = (bf16[1024,192]{1,0:T(8,128)(2,1)}, bf16[1024,576]{1,0:T(8,128)(2,1)}, f32[1,576]{1,0:T(1,128)}) custom-call(bf16[1024,768]{1,0:T(8,128)(2,1)} %bitcast.38, bf16[1024,768]{1,0:T(8,128)(2,1)} %bitcast.42, bf16[768,576]{1,0:T(8,128)(2,1)} %split.18.wq_ref, f32[1,576]{1,0:T(1,128)} %broadcast_in_dim.24.bq_ref, bf16[768,192]{1,0:T(8,128)(2,1)} %split.19.wo_ref, ...), custom_call_target="tpu_custom_call" | custom-call | tf_op jit(solution)/shard_map/attention/pallas_call | solution.py:549
  100.0 2.4 %convolution_convert_fusion.3 = bf16[768,192]{0,1:T(8,128)(2,1)} fusion(bf16[1024,768]{1,0:T(8,128)(2,1)S(1)} %bitcast.43, bf16[1024,192]{1,0:T(8,128)(2,1)} %get-tuple-element.29), kind=kOutput, calls=%fused_computation.13 | convolution fusion | flops 302137344 | bytes 2260992 | tf_op jit(solution)/shard_map/dot_general | solution.py:60
  102.4 1.9 copy.34
  104.3 3.5 %convolution_convert_fusion.2 = bf16[768,576]{0,1:T(8,128)(2,1)} fusion(bf16[1024,768]{1,0:T(8,128)(2,1)S(1)} %bitcast.39, bf16[1024,576]{1,0:T(8,128)(2,1)} %get-tuple-element.28), kind=kOutput, calls=%fused_computation.12 | convolution fusion | flops 906412032 | bytes 3637248 | tf_op jit(solution)/shard_map/dot_general | solution.py:60
  107.8 2.2 %copy.33 = bf16[768,576]{1,0:T(8,128)(2,1)} copy(bf16[768,576]{0,1:T(8,128)(2,1)} %convolution_convert_fusion.2) | data formatting | bytes 1769472 | tf_op jit(solution)/shard_map/convert_element_type | solution.py:624
  110.0 3.2 %multiply_convert_fusion = (bf16[1024,768]{1,0:T(8,128)(2,1)S(1)}, f32[1024,768]{1,0:T(8,128)S(1)}) fusion(f32[768]{0:T(1024)} %param.23, bf16[1024,768]{1,0:T(8,128)(2,1)S(1)} %bitcast.40, bf16[768,2304]{1,0:T(8,128)(2,1)} %bitcast.56), kind=kOutput, calls=%fused_computation.8 | convolution fusion | flops 1212678144 | bytes 7475200 | tf_op jit(solution)/shard_map/dot_general | solution.py:609
  113.3 4.1 %fusion.26 = (f32[768]{0:T(1024)S(1)}, bf16[1024,768]{1,0:T(8,128)(2,1)S(1)}) fusion(f32[1024,768]{1,0:T(8,128)S(1)} %get-tuple-element.74, f32[768]{0:T(1024)S(1)} %copy-done.25, bf16[1024,768]{1,0:T(8,128)(2,1)S(1)} %bitcast.44, bf16[768,2304]{1,0:T(8,128)(2,1)} %bitcast.57), kind=kOutput, calls=%fused_computation.71 | convolution fusion | flops 1217395968 | bytes 7477248 | tf_op jit(solution)/shard_map/dot_general | solution.py:611
  117.4 2.4 %convolution_convert_fusion = bf16[768,768]{1,0:T(8,128)(2,1)} fusion(bf16[1024,768]{1,0:T(8,128)(2,1)S(1)} %bitcast.45, bf16[1024,768]{1,0:T(8,128)(2,1)S(1)} %get-tuple-element.73), kind=kOutput, calls=%fused_computation.10 | convolution fusion | flops 1208549376 | bytes 4325376 | tf_op jit(solution)/shard_map/dot_general | solution.py:60
  119.8 2.6 %convolution_convert_fusion.1 = bf16[768,768]{1,0:T(8,128)(2,1)} fusion(bf16[1024,768]{1,0:T(8,128)(2,1)S(1)} %bitcast.41, bf16[1024,768]{1,0:T(8,128)(2,1)S(1)} %get-tuple-element.76), kind=kOutput, calls=%fused_computation.11 | convolution fusion | flops 1208549376 | bytes 4325376 | tf_op jit(solution)/shard_map/dot_general | solution.py:60
  122.5 1.3 concatenate.26.refs_7_
  123.8 3.3 %fusion.9 = f32[1024,768]{1,0:T(8,128)S(1)} fusion(bf16[1024,768]{1,0:T(8,128)(2,1)} %copy-done.28, bf16[768,2304]{1,0:T(8,128)(2,1)} %bitcast.58), kind=kOutput, calls=%fused_computation.21 | convolution fusion | flops 1207959552 | bytes 5898240 | tf_op jit(solution)/shard_map/dot_general | solution.py:66
  127.1 1.9 add_convert_fusion.1
  129.0 1.4 fusion.5
  130.5 2.6 %add_convert_fusion = bf16[1024,768]{1,0:T(8,128)(2,1)} fusion(f32[1024,768]{1,0:T(8,128)S(1)} %fusion.5, bf16[1024,576]{1,0:T(8,128)(2,1)S(1)} %copy-done.24, bf16[768,2304]{1,0:T(8,128)(2,1)S(1)} %bitcast.61), kind=kOutput, calls=%fused_computation.6 | convolution fusion | flops 907542528 | bytes 7012352 | tf_op jit(solution)/shard_map/dot_general | solution.py:66
  133.1 72.5 %scatter_all.1 = (f32[96,768]{1,0:T(8,128)}, f32[96,768]{1,0:T(8,128)}, f32[96,576]{1,0:T(8,128)}, f32[96,192]{1,0:T(8,128)}, f32[256,768]{1,0:T(8,128)}, /*index=5*/f32[256,768]{1,0:T(8,128)}, f32[16,768]{1,0:T(8,128)}) custom-call(bf16[8,96,768]{2,1,0:T(8,128)(2,1)} %bitcast.53, bf16[8,96,768]{2,1,0:T(8,128)(2,1)} %bitcast.52, ...), custom_call_target="tpu_custom_call" | custom-call | tf_op jit(solution)/shard_map/scatter_all/pallas_call | solution.py:382
  205.6 1.5 multiply_reduce_fusion.1
  207.2 2.4 %fusion.15 = (bf16[256,768]{1,0:T(8,128)(2,1)}, bf16[256,768]{1,0:T(8,128)(2,1)}) fusion(bf16[256,768]{1,0:T(8,128)(2,1)S(1)} %copy-done, f32[256,768]{1,0:T(8,128)S(1)} %copy-done.7, f32[256]{0:T(256)S(1)} %broadcast_multiply_fusion, f32[256]{0:T(256)S(1)} %broadcast_multiply_fusion.1, f32[768]{0:T(1024)S(1)} %copy-done.18, f32[256]{0:T(256)S(1)} %add_rsqrt_fusion, ...), kind=kLoop, calls=%fused_computation.29 | loop fusion | flops 2949120 | bytes 3159040 | tf_op jit(solution)/shard_map/convert_element_type | solution.py:662
  210.4 1.5 slice_reduce_fusion.1
  (92 shorter events, 9.6 us)
Async XLA Ops:
  0.6 8.7 %copy-start.14 = (bf16[768,96]{0,1:T(8,128)(2,1)S(1)}, bf16[768,96]{0,1:T(8,128)(2,1)}, u32[]{:S(2)}) copy-start(bf16[768,96]{0,1:T(8,128)(2,1)} %param.24) | copy-start | bytes 442372
  0.7 8.7 %copy-start.13 = (bf16[96,768]{1,0:T(8,128)(2,1)S(1)}, bf16[96,768]{1,0:T(8,128)(2,1)}, u32[]{:S(2)}) copy-start(bf16[96,768]{1,0:T(8,128)(2,1)} %param.22) | copy-start | bytes 442372
  0.7 8.6 %copy-start.15 = (bf16[96,576]{1,0:T(8,128)(2,1)S(1)}, bf16[96,576]{1,0:T(8,128)(2,1)}, u32[]{:S(2)}) copy-start(bf16[96,576]{1,0:T(8,128)(2,1)} %param.18) | copy-start | bytes 331780
  9.5 2.1 copy-start.17
  9.5 3.1 %copy-start.5 = (bf16[256,768]{1,0:T(8,128)(2,1)S(1)}, bf16[256,768]{1,0:T(8,128)(2,1)}, u32[]{:S(2)}) copy-start(bf16[256,768]{1,0:T(8,128)(2,1)} %param.13) | copy-start | bytes 1179652
  9.5 3.1 %copy-start.18 = (f32[768]{0:T(1024)S(1)}, f32[768]{0:T(1024)}, u32[]{:S(2)}) copy-start(f32[768]{0:T(1024)} %param.16) | copy-start | bytes 9220
  9.5 3.1 %copy-start.21 = (f32[768]{0:T(1024)S(1)}, f32[768]{0:T(1024)}, u32[]{:S(2)}) copy-start(f32[768]{0:T(1024)} %param.17) | copy-start | bytes 9220
  10.6 3.2 %copy-start = (bf16[256,768]{1,0:T(8,128)(2,1)S(1)}, bf16[256,768]{1,0:T(8,128)(2,1)}, u32[]{:S(2)}) copy-start(bf16[256,768]{1,0:T(8,128)(2,1)} %c_ref.1) | copy-start | bytes 1179652
  71.6 1.2 copy-start.1
  72.8 1.2 copy-start.3
  78.3 21.7 %copy-start.4 = (bf16[4,256,768]{2,1,0:T(8,128)(2,1)S(1)}, bf16[4,256,768]{2,1,0:T(8,128)(2,1)}, u32[]{:S(2)}) copy-start(bf16[4,256,768]{2,1,0:T(8,128)(2,1)} %copy-done.3) | copy-start | bytes 4718596
  100.0 4.3 %copy-start.2 = (bf16[4,256,768]{2,1,0:T(8,128)(2,1)S(1)}, bf16[4,256,768]{2,1,0:T(8,128)(2,1)}, u32[]{:S(2)}) copy-start(bf16[4,256,768]{2,1,0:T(8,128)(2,1)} %copy-done.1) | copy-start | bytes 4718596
  110.0 3.3 %copy-start.25 = (f32[768]{0:T(1024)S(1)}, f32[768]{0:T(1024)}, u32[]{:S(2)}) copy-start(f32[768]{0:T(1024)} %param.23) | copy-start | bytes 9220
  113.2 4.1 %copy-start.28 = (bf16[1024,768]{1,0:T(8,128)(2,1)}, bf16[1024,768]{1,0:T(8,128)(2,1)S(1)}, u32[]{:S(2)}) copy-start(bf16[1024,768]{1,0:T(8,128)(2,1)S(1)} %get-tuple-element.73) | copy-start | bytes 4718596
  117.4 2.5 %copy-start.26 = (bf16[1024,768]{1,0:T(8,128)(2,1)}, bf16[1024,768]{1,0:T(8,128)(2,1)S(1)}, u32[]{:S(2)}) copy-start(bf16[1024,768]{1,0:T(8,128)(2,1)S(1)} %get-tuple-element.76) | copy-start | bytes 4718596
  119.8 2.7 %copy-start.20 = (f32[1,768]{1,0:T(1,128)S(1)}, f32[1,768]{1,0:T(1,128)}, u32[]{:S(2)}) copy-start(f32[1,768]{1,0:T(1,128)} %broadcast_in_dim.50) | copy-start | bytes 9220
  123.8 3.3 %copy-start.8 = (bf16[8,96,2304]{2,1,0:T(8,128)(2,1)S(1)}, bf16[8,96,2304]{2,1,0:T(8,128)(2,1)}, u32[]{:S(2)}) copy-start(bf16[8,96,2304]{2,1,0:T(8,128)(2,1)} %get-tuple-element.27) | copy-start | bytes 10616836
  123.8 3.3 %copy-start.9 = (bf16[1024,192]{1,0:T(8,128)(2,1)S(1)}, bf16[1024,192]{1,0:T(8,128)(2,1)}, u32[]{:S(2)}) copy-start(bf16[1024,192]{1,0:T(8,128)(2,1)} %get-tuple-element.29) | copy-start | bytes 1179652
  127.1 1.9 copy-start.27
  129.0 1.4 copy-start.24
  133.1 72.5 %copy-start.6 = (bf16[256,768]{1,0:T(8,128)(2,1)S(1)}, bf16[256,768]{1,0:T(8,128)(2,1)}, u32[]{:S(2)}) copy-start(bf16[256,768]{1,0:T(8,128)(2,1)} %param.13) | copy-start | bytes 1179652
  133.1 74.1 %copy-start.22 = (f32[768]{0:T(1024)S(1)}, f32[768]{0:T(1024)}, u32[]{:S(2)}) copy-start(f32[768]{0:T(1024)} %param.25) | copy-start | bytes 9220
  133.1 74.1 %copy-start.23 = (f32[768]{0:T(1024)S(1)}, f32[768]{0:T(1024)}, u32[]{:S(2)}) copy-start(f32[768]{0:T(1024)} %param.21) | copy-start | bytes 9220
  205.6 1.6 copy-start.7
  207.2 6.0 %copy-start.16 = (f32[96,192]{1,0:T(8,128)S(1)}, f32[96,192]{1,0:T(8,128)}, u32[]{:S(2)}) copy-start(f32[96,192]{1,0:T(8,128)} %get-tuple-element.35) | copy-start | bytes 221188
  207.2 7.3 %copy-start.12 = (f32[96,576]{1,0:T(8,128)S(1)}, f32[96,576]{1,0:T(8,128)}, u32[]{:S(2)}) copy-start(f32[96,576]{1,0:T(8,128)} %get-tuple-element.125) | copy-start | bytes 663556
  207.2 8.0 %copy-start.11 = (f32[96,768]{1,0:T(8,128)S(1)}, f32[96,768]{1,0:T(8,128)}, u32[]{:S(2)}) copy-start(f32[96,768]{1,0:T(8,128)} %get-tuple-element.129) | copy-start | bytes 884740
  207.2 8.7 %copy-start.10 = (f32[96,768]{1,0:T(8,128)S(1)}, f32[96,768]{1,0:T(8,128)}, u32[]{:S(2)}) copy-start(f32[96,768]{1,0:T(8,128)} %get-tuple-element.37) | copy-start | bytes 884740
  211.9 4.7 %copy-start.19 = (f32[768]{0:T(1024)}, f32[768]{0:T(1024)S(1)}, u32[]{:S(2)}) copy-start(f32[768]{0:T(1024)S(1)} %get-tuple-element.128) | copy-start | bytes 9220
where the time goes:
time: 218 us; the launch traced here: 217 us
  Pallas kernels  151 us (69%)
  matrix products  27.5 us (13%)
  local copies, waits for them, and re-layouts  25.2 us (12%)
  other arithmetic  11.5 us (5%)
    pallas_call x1, Pallas kernels, scatter_all(): pl.pallas_call(functools.partial(scatter_kernel, fsdp, tp, many), out_sha...  72.5 us
    pallas_call x1, Pallas kernels, gather_all(): pl.pallas_call(functools.partial(gather_kernel, fsdp, tp), out_shape=shap...  57.8 us
    pallas_call x1, Pallas kernels, attention_branch(): pl.pallas_call(functools.partial(attention_kernel, heads), out_shape=(jax...  21 us
    dot_general x4, matrix products, cross_rows(): lax.dot_general(left, right, (((0,), (0,)), ((), ())), preferred_element_...  10.9 us
    dot_general x4, matrix products, cross_cols(): lax.dot_general(left, right, (((1,), (1,)), ((), ())), preferred_element_...  9.25 us
    unnamed x64, local copies, waits for them, and re-layouts  6.79 us

commit v1 on v0

--- a/solution.py
+++ b/solution.py
@@ -578,7 +578,7 @@
     return mixed_rows, packed_grad, sums[0]
 
 
-def body(
+def staged_body(
     layer_input,
     out_cotangent,
     segments,
@@ -676,6 +676,817 @@
     )
 
 
+DOCS = 4
+
+
+def error_function(value):
+    x = jnp.clip(value, -3.7439211627767994, 3.7439211627767994)
+    y = x * x
+    top = jnp.float32(0.00022905065861350646)
+    for c in (
+        0.0034082910107109506,
+        0.050955695062380861,
+        0.18520832239976145,
+        1.128379143519084,
+    ):
+        top = top * y + jnp.float32(c)
+    low = jnp.float32(-1.1791602954361697e-7)
+    for c in (
+        0.000023547966471313185,
+        0.0010179625278914885,
+        0.014070470171167667,
+        0.11098505178285362,
+        0.49746925110067538,
+        1.0,
+    ):
+        low = low * y + jnp.float32(c)
+    return x * top / low
+
+
+def layer_kernel(
+    fsdp,
+    tp,
+    heads,
+    x_ref,
+    c_ref,
+    seg_ref,
+    gain_ref,
+    shift_ref,
+    ob_ref,
+    db_ref,
+    bq_ref,
+    bu_ref,
+    wq_ref,
+    wo_ref,
+    wu_ref,
+    wd_ref,
+    y_out,
+    dx_out,
+    gq_out,
+    go_out,
+    gu_out,
+    gd_out,
+    v_out,
+    w_all,
+    h_all,
+    c_all,
+    h_turn,
+    c_turn,
+    normed_ref,
+    inverse_ref,
+    cos_ref,
+    sin_a,
+    sin_b,
+    start_ref,
+    qkv_ref,
+    do_ref,
+    queries,
+    keys_in,
+    values_in,
+    grads_in,
+    mixed,
+    grad_q,
+    grad_k,
+    grad_v,
+    o_ref,
+    packed,
+    gelu_ref,
+    pre_ref,
+    g_all,
+    halves,
+    joined,
+    lands,
+    part,
+    mates,
+    summed,
+    sides_in,
+    d_out,
+    early,
+    early_all,
+    rows,
+    rows_all,
+    shared,
+    up_send,
+    down_send,
+    z_recv,
+    y_send,
+    y_recv,
+    x_send,
+    x_recv,
+    m_send,
+    m_recv,
+    a_send,
+    a_recv,
+    l_send,
+    l_recv,
+    pm_send,
+    pm_recv,
+    px_send,
+    px_recv,
+    e_send,
+    e_recv,
+    v_send,
+    v_recv,
+    u_send,
+    u_recv,
+):
+    f32 = jnp.float32
+    bf16 = jnp.bfloat16
+    f, t, pair, line = place(fsdp, tp)
+    lines = fsdp // 2
+    sides = tp // 2
+    side = lax.div(t, 2)
+    par = lax.rem(t, 2)
+    partner = 2 * line + 1 - pair
+    mate = 2 * side + 1 - par
+    block = x_ref.shape[0]
+    model = x_ref.shape[1]
+    shard = wu_ref.shape[0]
+    hidden = wu_ref.shape[1]
+    wide = wq_ref.shape[1]
+    length = tp * block
+    two = 2 * HEAD_DIM
+    scale = HEAD_DIM ** (-0.5)
+    half = ROT // 2
+
+    barrier = pltpu.get_barrier_semaphore()
+    each(
+        1,
+        fsdp,
+        lambda step: pl.semaphore_signal(
+            barrier, inc=1, device_id=(lax.rem(f + step, fsdp), t), device_id_type=MESH
+        ),
+    )
+    each(
+        1,
+        tp,
+        lambda step: pl.semaphore_signal(
+            barrier, inc=1, device_id=(f, lax.rem(t + step, tp)), device_id_type=MESH
+        ),
+    )
+    w_all[0, f] = jnp.concatenate([wq_ref[...], wo_ref[...]], axis=1)
+    w_all[1, f] = wu_ref[...]
+    w_all[2, f] = wd_ref[...]
+    c_all[t] = c_ref[...]
+    own = x_ref[...].astype(f32)
+    normed, inverse, shifted = layer_norm(own, gain_ref[...], shift_ref[...])
+    h_all[t] = shifted.astype(bf16)
+    normed_ref[...] = normed
+    inverse_ref[...] = inverse
+    pl.semaphore_wait(barrier, fsdp + tp - 2)
+
+    def slot(origin):
+        return 2 * origin + pair
+
+    def z_copy(i, origin, send, to):
+        view = w_all.at[i, slot(origin)]
+        return remote(view, view, send.at[i, origin], z_recv.at[i, origin], (2 * to + pair, t))
+
+    def z_up(i, origin):
+        return z_copy(i, origin, up_send, line + 1)
+
+    def z_down(i, origin):
+        return z_copy(i, origin, down_send, line - 1)
+
+    def y_copy(i, origin, side_of):
+        view = w_all.at[i, 2 * origin + side_of]
+        return remote(view, view, y_send.at[i, origin], y_recv.at[i, origin], (partner, t))
+
+    def send_own(i):
+        @pl.when(line + 1 < lines)
+        def _():
+            z_up(i, line).start()
+
+        @pl.when(line > 0)
+        def _():
+            z_down(i, line).start()
+
+        y_copy(i, line, pair).start()
+
+    def relay(r):
+        i = lax.div(r, lines - 1)
+        k = lax.rem(r, lines - 1) + 1
+        below = line - k
+        above = line + k
+
+        @pl.when(below >= 0)
+        def _():
+            z_up(i, below).wait_recv()
+
+            @pl.when(line + 1 < lines)
+            def _():
+                z_up(i, below).start()
+
+            y_copy(i, below, pair).start()
+
+        @pl.when(above < lines)
+        def _():
+            z_down(i, above).wait_recv()
+
+            @pl.when(line > 0)
+            def _():
+                z_down(i, above).start()
+
+            y_copy(i, above, pair).start()
+
+    relays = 3 * (lines - 1)
+
+    tokens = (h_all, c_all)
+
+    def x_copy(which, step, place_of):
+        view = tokens[which].at[place_of]
+        other = lax.rem(side + step, sides)
+        return remote(
+            view, view, x_send.at[which, step], x_recv.at[which, step], (f, 2 * other + par)
+        )
+
+    def m_copy(which, origin, parity):
+        view = tokens[which].at[2 * origin + parity]
+        return remote(
+            view, view, m_send.at[which, origin], m_recv.at[which, origin], (f, mate)
+        )
+
+    def arrive(which):
+        def one(step):
+            origin = lax.rem(side + sides - step, sides)
+            x_copy(which, step, 2 * origin + par).wait_recv()
+            m_copy(which, origin, par).start()
+
+        each(1, sides, one)
+
+    def settle(which):
+        each(0, sides, lambda origin: m_copy(which, origin, 1 - par).wait_recv())
+
+    each(1, sides, lambda step: x_copy(0, step, t).start())
+    send_own(0)
+    m_copy(0, side, par).start()
+    each(1, sides, lambda step: x_copy(1, step, t).start())
+    m_copy(1, side, par).start()
+    send_own(1)
+
+    seg = seg_ref[...]
+    down_rows = lax.broadcasted_iota(jnp.int32, (length, 1), 0)
+    along_row = lax.broadcasted_iota(jnp.int32, (1, length), 1)
+    start_col = jnp.zeros((length, 1), jnp.int32)
+    start_row = jnp.zeros((1, length), jnp.int32)
+    for d in range(1, DOCS):
+        count = jnp.sum((seg < d).astype(jnp.int32), axis=1, keepdims=True)
+        start_col = jnp.where(down_rows >= count, count, start_col)
+        start_row = jnp.where(along_row >= count, count, start_row)
+    start_ref[...] = start_col
+    spot = (along_row - start_row).astype(f32)
+    order = lax.broadcasted_iota(jnp.int32, (half, 1), 0).astype(f32)
+    rates = jnp.exp(order * (-2.0 / ROT * 9.210340371976184))
+    angles = spot * rates
+    lane = lax.broadcasted_iota(jnp.int32, (half, two), 1) % HEAD_DIM
+    pick = lax.broadcasted_iota(jnp.int32, (half, two), 0)
+    first_half = (lane == pick).astype(f32)
+    last_half = (lane == pick + half).astype(f32)
+
+    def spread_out(table, matrix):
+        return lax.dot_general(
+            table,
+            matrix,
+            (((0,), (0,)), ((), ())),
+            precision=lax.Precision.HIGHEST,
+            preferred_element_type=f32,
+        )
+
+    cosine = jnp.cos(angles)
+    sine = jnp.sin(angles)
+    beyond = lax.broadcasted_iota(jnp.int32, (1, two), 1) % HEAD_DIM >= ROT
+    cos_ref[...] = jnp.where(beyond, 1.0, spread_out(cosine, first_half + last_half))
+    sin_a[...] = spread_out(sine, last_half)
+    sin_b[...] = -spread_out(sine, first_half)
+
+    each(0, lines - 1, relay)
+    send_own(2)
+    arrive(0)
+    ahead_of = (lines - 1) + min(2, lines - 1)
+    relay(lines - 1)
+    settle(0)
+    for s in range(tp):
+        h_turn[:, s * block : (s + 1) * block] = h_all[s].T
+    each(lines, ahead_of, relay)
+    each(0, lines, lambda origin: y_copy(0, origin, 1 - pair).wait_recv())
+
+    def project_q(s, carry):
+        weight = w_all[0].reshape(model, model)
+        part_of = pl.ds(s * block, block)
+        qkv_ref[part_of] = (
+            jnp.dot(h_all[s], weight[:, :wide], preferred_element_type=f32) + bq_ref[...]
+        )
+        return carry
+
+    lax.fori_loop(0, tp, project_q, 0)
+    arrive(1)
+
+    def rotated(value, spots, sign):
+        return (
+            value * cos_ref[spots]
+            + sign
+            * (
+                pltpu.roll(value, half, 1) * sin_a[spots]
+                + pltpu.roll(value, two - half, 1) * sin_b[spots]
+            )
+        )
+
+    for n in range(heads):
+        base = 3 * HEAD_DIM * n
+
+        def prepare(s, carry, n=n, base=base):
+            spots = pl.ds(s * block, block)
+            both = rotated(qkv_ref[spots, base : base + two], spots, 1.0)
+            queries[n, spots] = both[:, :HEAD_DIM].astype(bf16) * bf16(scale)
+            keys_in[n, spots] = both[:, HEAD_DIM:].astype(bf16)
+            values_in[n, spots] = qkv_ref[spots, base + two : base + two + HEAD_DIM].astype(bf16)
+            return carry
+
+        lax.fori_loop(0, tp, prepare, 0)
+    settle(1)
+    for s in range(tp):
+        c_turn[:, s * block : (s + 1) * block] = c_all[s].T
+
+    def project_o(s, carry):
+        weight = w_all[0].reshape(model, model)
+        spots = pl.ds(s * block, block)
+        value = jnp.dot(c_all[s], weight[:, wide:], preferred_element_type=f32).astype(bf16)
+        for n in range(heads):
+            grads_in[n, spots] = value[:, n * HEAD_DIM : (n + 1) * HEAD_DIM]
+        return carry
+
+    lax.fori_loop(0, tp, project_o, 0)
+    grad_k[...] = jnp.zeros_like(grad_k)
+    grad_v[...] = jnp.zeros_like(grad_v)
+    span = min(SPAN, length)
+    parts = length // span
+    steps = heads * parts
+    busy = max(1, steps * 3 // 4)
+    left = relays - ahead_of
+
+    def due(j):
+        return ahead_of + jnp.minimum(left, lax.div(j * left, busy))
+
+    def one_head(n, carry):
+        for m in range(parts):
+            first = m * span
+            last = first + span
+            low = max(0, (first - MOST) // span * span)
+            spots = slice(first, last)
+            window = slice(low, last)
+            q = queries[n, spots]
+            k = keys_in[n, window]
+            v = values_in[n, window]
+            g = grads_in[n, spots]
+            shape = (span, last - low)
+            key_at = lax.broadcasted_iota(jnp.int32, shape, 1) + low
+            allowed = (key_at >= start_ref[spots]) & (
+                lax.broadcasted_iota(jnp.int32, shape, 0) + first >= key_at
+            )
+            scores = jnp.where(allowed, cross_cols(q, k), -1e30)
+            exps = jnp.exp(scores - jnp.max(scores, axis=-1, keepdims=True))
+            probs = exps * (1.0 / jnp.sum(exps, axis=-1, keepdims=True))
+            weights = probs.astype(bf16)
+            out = jnp.dot(weights, v, preferred_element_type=f32).astype(bf16)
+            mixed[n, spots] = out
+            delta = jnp.sum(g.astype(f32) * out.astype(f32), axis=-1, keepdims=True)
+            grad_probs = cross_cols(g, v)
+            grad_scores = (probs * (grad_probs - delta)).astype(bf16)
+            grad_q[n, spots] = jnp.dot(grad_scores, k, preferred_element_type=f32) * scale
+            grad_k[n, window] += cross_rows(grad_scores, q)
+            grad_v[n, window] += cross_rows(weights, g)
+            j = n * parts + m
+            each(due(j), due(j + 1), relay)
+        return carry
+
+    lax.fori_loop(0, heads, one_head, 0)
+
+    early[...] = jnp.zeros_like(early)
+
+    def finish(s, carry):
+        spots = pl.ds(s * block, block)
+        pieces = []
+        for n in range(heads):
+            both = jnp.concatenate([grad_q[n, spots], grad_k[n, spots]], axis=1)
+            pieces += [rotated(both, spots, -1.0), grad_v[n, spots]]
+        whole = jnp.concatenate(pieces, axis=1)
+        early[0:1, :wide] += jnp.sum(whole, axis=0, keepdims=True)
+        packed[spots] = whole.astype(bf16)
+        o_ref[spots] = jnp.concatenate([mixed[n, spots] for n in range(heads)], axis=1)
+        return carry
+
+    lax.fori_loop(0, tp, finish, 0)
+
+    def ahead(step):
+        return lax.rem(line + step, lines)
+
+    def across(i, step):
+        return remote(
+            g_all.at[i, 2 * ahead(step) + 1 - pair],
+            halves.at[i, step],
+            a_send.at[i, step],
+            a_recv.at[i, step],
+            (partner, t),
+        )
+
+    def along(i, step):
+        return remote(
+            joined.at[i, step],
+            lands.at[i, step],
+            l_send.at[i, step],
+            l_recv.at[i, step],
+            (2 * ahead(step) + pair, t),
+        )
+
+    def start_across(i):
+        each(1, lines, lambda step: across(i, step).start())
+        across(i, 0).start()
+
+    def join(i, step):
+        across(i, step).wait_recv()
+        joined[i, step] = (
+            g_all[i, 2 * ahead(step) + pair].astype(f32) + halves[i, step].astype(f32)
+        ).astype(bf16)
+        along(i, step).start()
+
+    tile = model // 2
+    many = tile // shard
+
+    def store_grad(i, j, value):
+        g_all[i, pl.ds(j * many, many)] = value.astype(bf16).reshape(many, shard, value.shape[1])
+
+    def grad_attention(j, carry):
+        spots = pl.ds(j * tile, tile)
+        store_grad(
+            0,
+            j,
+            jnp.concatenate(
+                [
+                    jnp.dot(h_turn[spots], packed[...], preferred_element_type=f32),
+                    jnp.dot(c_turn[spots], o_ref[...], preferred_element_type=f32),
+                ],
+                axis=1,
+            ),
+        )
+        return carry
+
+    def grad_up(j, carry):
+        store_grad(
+            1,
+            j,
+            jnp.dot(h_turn[pl.ds(j * tile, tile)], pre_ref[...], preferred_element_type=f32),
+        )
+        return carry
+
+    def grad_down(j, carry):
+        store_grad(
+            2,
+            j,
+            jnp.dot(c_turn[pl.ds(j * tile, tile)], gelu_ref[...], preferred_element_type=f32),
+        )
+        return carry
+
+    lax.fori_loop(0, 2, grad_attention, 0)
+    start_across(0)
+
+    each(due(steps), relays, relay)
+    each(0, lines, lambda origin: y_copy(1, origin, 1 - pair).wait_recv())
+    each(0, lines, lambda origin: y_copy(2, origin, 1 - pair).wait_recv())
+
+    def hidden_rows(s, carry):
+        spots = pl.ds(s * block, block)
+        up = w_all[1].reshape(model, hidden)
+        down = w_all[2].reshape(model, hidden)
+        a = jnp.dot(h_all[s], up, preferred_element_type=f32) + bu_ref[...]
+        bell = 0.5 * (1.0 + error_function(a * 0.7071067811865476))
+        gelu_ref[spots] = (a * bell).astype(bf16)
+        slope = bell + a * jnp.exp(-0.5 * a * a) * 0.3989422804014327
+        grad = jnp.dot(c_all[s], down, preferred_element_type=f32) * slope
+        early[1:2, :hidden] += jnp.sum(grad, axis=0, keepdims=True)
+        pre_ref[spots] = grad.astype(bf16)
+        return carry
+
+    lax.fori_loop(0, tp, hidden_rows, 0)
+
+    def e_copy(step, place_of):
+        return remote(
+            early,
+            early_all.at[place_of],
+            e_send.at[step],
+            e_recv.at[step],
+            (lax.rem(f + step, fsdp), t),
+        )
+
+    early[2:3] = jnp.sum(c_all[t].astype(f32), axis=0, keepdims=True)
+    join(0, 1)
+    lax.fori_loop(0, 2, grad_up, 0)
+    start_across(1)
+    each(1, fsdp, lambda step: e_copy(step, f).start())
+    join(0, 2)
+
+    def pm_copy(which, origin):
+        return remote(
+            part.at[which, 2 * origin + 1 - par],
+            mates.at[which, origin],
+            pm_send.at[which, origin],
+            pm_recv.at[which, origin],
+            (f, mate),
+        )
+
+    def px_copy(which, step):
+        other = lax.rem(side + step, sides)
+        return remote(
+            summed.at[which, step],
+            sides_in.at[which, step],
+            px_send.at[which, step],
+            px_recv.at[which, step],
+            (f, 2 * other + par),
+        )
+
+    def feature_rows(s, carry):
+        spots = pl.ds(s * block, block)
+        weight = w_all[0].reshape(model, model)
+        part[0, s] = (
+            cross_cols(packed[spots], weight[:, :wide])
+            + cross_cols(pre_ref[spots], w_all[1].reshape(model, hidden))
+        ).astype(bf16)
+        return carry
+
+    def branch_rows(s, carry):
+        spots = pl.ds(s * block, block)
+        weight = w_all[0].reshape(model, model)
+        part[1, s] = (
+            cross_cols(o_ref[spots], weight[:, wide:])
+            + cross_cols(gelu_ref[spots], w_all[2].reshape(model, hidden))
+        ).astype(bf16)
+        return carry
+
+    def pass_on(which):
+        def one(step):
+            other = lax.rem(side + step, sides)
+            pm_copy(which, other).wait_recv()
+            summed[which, step] = (
+                part[which, 2 * other + par].astype(f32) + mates[which, other].astype(f32)
+            ).astype(bf16)
+            px_copy(which, step).start()
+
+        each(1, sides, one)
+
+    def gathered(which):
+        pm_copy(which, side).wait_recv()
+        d_out[...] = part[which, t].astype(f32) + mates[which, side].astype(f32)
+
+        def one(step):
+            px_copy(which, step).wait_recv()
+            d_out[...] += sides_in[which, step].astype(f32)
+
+        each(1, sides, one)
+
+    lax.fori_loop(0, tp, feature_rows, 0)
+    each(0, sides, lambda origin: pm_copy(0, origin).start())
+    each(3, lines, lambda step: join(0, step))
+    lax.fori_loop(0, 2, grad_down, 0)
+    start_across(2)
+    pass_on(0)
+    lax.fori_loop(0, tp, branch_rows, 0)
+    each(0, sides, lambda origin: pm_copy(1, origin).start())
+    join(1, 1)
+    pass_on(1)
+    each(2, lines, lambda step: join(1, step))
+
+    gathered(0)
+    rows[...] = jnp.zeros_like(rows)
+    rows[0:1] = jnp.sum(d_out[...] * normed_ref[...], axis=0, keepdims=True)
+    rows[1:2] = jnp.sum(d_out[...], axis=0, keepdims=True)
+    each(1, fsdp, lambda step: e_copy(step, lax.rem(f + fsdp - step, fsdp)).wait_recv())
+    early_all[f] = early[...]
+    total = lax.fori_loop(1, fsdp, lambda step, value: value + early_all[step], early_all[0])
+    v_out[8:16] = total
+    rows[2:3] = early[2:3]
+
+    def v_copy(step, place_of):
+        return remote(
+            rows,
+            rows_all.at[place_of],
+            v_send.at[step],
+            v_recv.at[step],
+            (lax.rem(f + step, fsdp), t),
+        )
+
+    each(1, fsdp, lambda step: v_copy(step, f).start())
+    rows_all[f] = rows[...]
+    normed = normed_ref[...]
+    scaled = d_out[...] * gain_ref[...]
+    dx_out[...] = (
+        c_ref[...].astype(f32)
+        + inverse_ref[...]
+        * (
+            scaled
+            - jnp.mean(scaled, axis=-1, keepdims=True)
+            - normed * jnp.mean(scaled * normed, axis=-1, keepdims=True)
+        )
+    ).astype(bf16)
+    join(2, 1)
+    each(1, fsdp, lambda step: v_copy(step, lax.rem(f + fsdp - step, fsdp)).wait_recv())
+    shared[t] = lax.fori_loop(1, fsdp, lambda step, value: value + rows_all[step], rows_all[0])
+
+    def u_copy(step, place_of):
+        view = shared.at[place_of]
+        return remote(
+            shared.at[t],
+            view,
+            u_send.at[step],
+            u_recv.at[step],
+            (f, lax.rem(t + step, tp)),
+        )
+
+    each(1, tp, lambda step: u_copy(step, t).start())
+    each(2, lines, lambda step: join(2, step))
+    gathered(1)
+    y_out[...] = (x_ref[...].astype(f32) + d_out[...] + ob_ref[...] + db_ref[...]).astype(bf16)
+    each(1, tp, lambda step: u_copy(step, lax.rem(t + tp - step, tp)).wait_recv())
+    whole = shared[0]
+    for step in range(1, tp):
+        whole = whole + shared[step]
+    v_out[0:8] = whole
+
+    def collected(i):
+        across(i, 0).wait_recv()
+        value = g_all[i, f].astype(f32) + halves[i, 0].astype(f32)
+
+        def one(step, value):
+            along(i, step).wait_recv()
+            return value + lands[i, step].astype(f32)
+
+        return lax.fori_loop(1, lines, one, value)
+
+    value = collected(0)
+    gq_out[...] = value[:, :wide]
+    go_out[...] = value[:, wide:]
+    gu_out[...] = collected(1)
+    gd_out[...] = collected(2)
+
+    for i in range(3):
+
+        @pl.when(line + 1 < lines)
+        def _():
+            each(0, line + 1, lambda origin: z_up(i, origin).wait_send())
+
+        @pl.when(line > 0)
+        def _():
+            each(line, lines, lambda origin: z_down(i, origin).wait_send())
+
+        each(0, lines, lambda origin: y_copy(i, origin, pair).wait_send())
+        each(0, lines, lambda step: across(i, step).wait_send())
+        each(1, lines, lambda step: along(i, step).wait_send())
+    for which in range(2):
+        each(1, sides, lambda step: x_copy(which, step, t).wait_send())
+        each(0, sides, lambda origin: m_copy(which, origin, par).wait_send())
+        each(0, sides, lambda origin: pm_copy(which, origin).wait_send())
+        each(1, sides, lambda step: px_copy(which, step).wait_send())
+    each(1, fsdp, lambda step: e_copy(step, f).wait_send())
+    each(1, fsdp, lambda step: v_copy(step, f).wait_send())
+    each(1, tp, lambda step: u_copy(step, t).wait_send())
+
+
+def layer_call(x, c, seg, gain, shift, ob, db, bq, bu, wq, wo, wu, wd):
+    fsdp = lax.axis_size("fsdp")
+    tp = lax.axis_size("tp")
+    lines = fsdp // 2
+    sides = tp // 2
+    block, model = x.shape
+    shard, hidden = wu.shape
+    wide = wq.shape[1]
+    heads = wide // (3 * HEAD_DIM)
+    length = tp * block
+    two = 2 * HEAD_DIM
+    f32 = jnp.float32
+    bf16 = jnp.bfloat16
+    vmem = pl.BlockSpec(memory_space=pltpu.VMEM)
+    dma = pltpu.SemaphoreType.DMA
+    buf = pltpu.VMEM
+    return pl.pallas_call(
+        functools.partial(layer_kernel, fsdp, tp, heads),
+        out_shape=(
+            jax.ShapeDtypeStruct((block, model), bf16),
+            jax.ShapeDtypeStruct((block, model), bf16),
+            jax.ShapeDtypeStruct((shard, wide), f32),
+            jax.ShapeDtypeStruct((shard, model - wide), f32),
+            jax.ShapeDtypeStruct((shard, hidden), f32),
+            jax.ShapeDtypeStruct((shard, hidden), f32),
+            jax.ShapeDtypeStruct((16, model), f32),
+        ),
+        in_specs=[vmem] * 13,
+        out_specs=(vmem,) * 7,
+        scratch_shapes=[
+            buf((3, fsdp, shard, model), bf16),
+            buf((tp, block, model), bf16),
+            buf((tp, block, model), bf16),
+            buf((model, length), bf16),
+            buf((model, length), bf16),
+            buf((block, model), f32),
+            buf((block, 1), f32),
+            buf((length, two), f32),
+            buf((length, two), f32),
+            buf((length, two), f32),
+            buf((length, 1), jnp.int32),
+            buf((length, wide), f32),
+            buf((8, 128), f32),
+        ]
+        + [buf((heads, length, HEAD_DIM), bf16)] * 5
+        + [buf((heads, length, HEAD_DIM), f32)] * 3
+        + [
+            buf((length, heads * HEAD_DIM), bf16),
+            buf((length, wide), bf16),
+            buf((length, hidden), bf16),
+            buf((length, hidden), bf16),
+            buf((3, fsdp, shard, model), bf16),
+            buf((3, lines, shard, model), bf16),
+            buf((3, lines, shard, model), bf16),
+            buf((3, lines, shard, model), bf16),
+            buf((2, tp, block, model), bf16),
+            buf((2, sides, block, model), bf16),
+            buf((2, sides, block, model), bf16),
+            buf((2, sides, block, model), bf16),
+            buf((block, model), f32),
+            buf((8, model), f32),
+            buf((fsdp, 8, model), f32),
+            buf((8, model), f32),
+            buf((fsdp, 8, model), f32),
+            buf((tp, 8, model), f32),
+        ]
+        + [dma((3, lines))] * 5
+        + [dma((2, sides))] * 4
+        + [dma((3, lines))] * 4
+        + [dma((2, sides))] * 4
+        + [dma((fsdp,))] * 4
+        + [dma((tp,))] * 2,
+        compiler_params=pltpu.CompilerParams(
+            collective_id=3, has_side_effects=True, vmem_limit_bytes=62 * 1024 * 1024
+        ),
+        name="layer",
+    )(x, c, seg, gain, shift, ob, db, bq, bu, wq, wo, wu, wd)
+
+
+def fused_body(
+    layer_input,
+    out_cotangent,
+    segments,
+    norm_gain,
+    norm_bias,
+    qkv_weight,
+    qkv_bias,
+    out_weight,
+    out_bias,
+    up_weight,
+    up_bias,
+    down_weight,
+    down_bias,
+):
+    y, dx, qkv_grad, out_grad, up_grad, down_grad, sums = layer_call(
+        layer_input,
+        out_cotangent,
+        segments,
+        norm_gain[None],
+        norm_bias[None],
+        out_bias[None],
+        down_bias[None],
+        qkv_bias[None],
+        up_bias[None],
+        qkv_weight,
+        out_weight.T,
+        up_weight,
+        down_weight.T,
+    )
+    return (
+        y,
+        dx,
+        sums[0],
+        sums[1],
+        qkv_grad,
+        sums[8, : qkv_bias.shape[0]],
+        out_grad.T,
+        sums[2],
+        up_grad,
+        sums[9, : up_bias.shape[0]],
+        down_grad.T,
+        sums[2],
+    )
+
+
+def body(*args):
+    rows = args[5].shape[0]
+    model, hidden = args[9].shape[0] * lax.axis_size("fsdp"), args[9].shape[1]
+    fits = (
+        rows % 16 == 0
+        and (model // 2) % rows == 0
+        and args[5].shape[1] + args[7].shape[0] == model == hidden
+        and args[2].shape == (1, lax.axis_size("tp") * args[0].shape[0])
+        and args[0].shape[0] == SPAN
+    )
+    return fused_body(*args) if fits else staged_body(*args)
+
+
 def solution(mesh):
     in_specs = (
         P(("fsdp", "tp"), None),

time: 218 us -> 126 us (0.58)
  Pallas kernels: 151 us -> 108 us
  matrix products: 27.5 us -> 0 us
  other arithmetic: 11.5 us -> 0 us
  local copies, waits for them, and re-layouts: 25.2 us -> 16.3 us
    pallas_call x3 -> x1, Pallas kernels: 151 us -> 108 us  [layer_call(): pl.pallas_call(functools.partial(layer_kernel, fsdp, tp, heads), out_shap...]
    dot_general x10 -> x0, matrix products: 27.5 us -> none  [the longest x4 10.9 us: cross_rows(): lax.dot_general(left, right, (((0,), (0,)), ((), ())), preferred_element_...]
    reduce_sum x4 -> x0, other arithmetic: 4.95 us -> none  [the longest x1 1.51 us: body(): jnp.mean(scaled, axis=-1, keepdims=True)]
    split x2 -> x0, local copies, waits for them, and re-layouts: 4.26 us -> none  [body(): full_up, full_down, full_qkv, full_out = jnp.split(w_all, ends, axis=1)]
    convert_element_type x2 -> x0, local copies, waits for them, and re-layouts: 4.1 us -> none  [the longest x1 2.23 us: body(): cross_rows(features, packed_bf).astype(jnp.bfloat16)]
    another operation x6 -> x0, local copies, waits for them, and re-layouts: 3.25 us -> none  [the longest x2 1.08 us: attention_branch(): cos_full = jnp.tile(jnp.pad(cos_table, rest, constant_values=1.0), (1, 2))]
    unnamed x64 -> x30, local copies, waits for them, and re-layouts: 6.79 us -> 10 us
    convert_element_type x2 -> x0, other arithmetic: 2.52 us -> none  [the longest x1 2.44 us: body(): input_grad = (cot_rows + inverse * (scaled - jnp.mean(scaled, axis=-1, ke...]
where the time goes in v1:
time: 126 us; the launch traced here: 125 us
  Pallas kernels  108 us (86%)
  local copies, waits for them, and re-layouts  16.3 us (13%)
    pallas_call x1, Pallas kernels, layer_call(): pl.pallas_call(functools.partial(layer_kernel, fsdp, tp, heads), out_shap...  108 us
    unnamed x30, local copies, waits for them, and re-layouts  10 us

profile of v1, /device:TPU:0, one launch (start us, length us, event | category | flops | bytes accessed | tf_op | source)
XLA Modules:
  0.0 125.2 jit_solution(5991739992740976269)
XLA Ops:
  0.6 0.0 copy-start.5
  0.7 1.5 %copy.25 = bf16[192,96]{0,1:T(8,128)(2,1)} copy(bf16[192,96]{1,0:T(8,128)(2,1)} %param.20) | data formatting | bytes 73728 | tf_op args[7]
  2.2 0.0 copy-start.6
  2.2 0.0 copy-done.5
  2.2 0.6 broadcast_in_dim.18.gain_ref
  2.8 0.1 copy-done.6
  2.9 0.0 copy-start.7
  2.9 0.6 broadcast_in_dim.19.shift_ref
  3.4 0.1 copy-done.7
  3.6 0.0 copy-start.8
  3.6 0.6 broadcast_in_dim.20.ob_ref
  4.1 0.1 copy-done.8
  4.2 0.6 broadcast_in_dim.21.db_ref
  4.8 0.1 copy-done.9
  4.9 0.6 broadcast_in_dim.23.bu_ref
  5.5 0.1 copy-done.10
  5.6 0.6 broadcast_in_dim.22.bq_ref
  6.2 108.2 %layer.1 = (bf16[256,768]{1,0:T(8,128)(2,1)}, bf16[256,768]{1,0:T(8,128)(2,1)}, f32[96,576]{1,0:T(8,128)}, f32[96,192]{1,0:T(8,128)}, f32[96,768]{1,0:T(8,128)}, /*index=5*/f32[96,768]{1,0:T(8,128)}, f32[16,768]{1,0:T(8,128)}) custom-call(bf16[256,768]{1,0:T(8,128)(2,1)} %x_ref.1, bf16[256,768]{1,0:T(8,128)(2,1)} %c_ref.1, s32[1,1024]{1,0:T(1,128)} %seg_ref.1, ...), custom_call_target="tpu_custom_call" | custom-call | tf_op jit(solution)/shard_map/layer/pallas_call | solution.py:1368
  114.4 1.5 %slice_reduce_fusion = (f32[768]{0:T(1024)}, f32[768]{0:T(1024)S(1)}, f32[768]{0:T(1024)}, f32[768]{0:T(1024)}) fusion(f32[16,768]{1,0:T(8,128)} %get-tuple-element.21), kind=kLoop, calls=%fused_computation | loop fusion | bytes 24576 | tf_op jit(solution)/shard_map/slice | solution.py:1471
  115.9 1.3 %slice_reduce_fusion.4 = f32[576]{0:T(1024)} fusion(f32[16,768]{1,0:T(8,128)} %get-tuple-element.21), kind=kLoop, calls=%fused_computation.4 | loop fusion | bytes 4608 | tf_op jit(solution)/shard_map/slice | solution.py:1467
  117.3 1.6 %copy.26 = f32[192,96]{1,0:T(8,128)} copy(f32[192,96]{0,1:T(8,128)} %bitcast.7) | data formatting | bytes 147456
  118.9 0.0 copy-done.4
  118.9 0.6 copy.33
  119.5 1.8 %copy.34 = bf16[256,768]{1,0:T(8,128)(2,1)} copy(bf16[256,768]{1,0:T(8,128)(2,1)} %get-tuple-element.78) | data formatting | bytes 786432
  121.3 0.0 copy-done
  121.3 0.7 copy.35
  122.1 0.3 copy-done.3
  122.4 0.7 copy.36
  123.1 0.4 copy-done.2
  123.4 0.7 copy.37
  124.2 0.4 copy-done.1
  124.5 0.7 copy.38
  (7 shorter events, 0.0 us)
Async XLA Ops:
  0.6 1.5 %copy-start.5 = (f32[768]{0:T(1024)S(1)}, f32[768]{0:T(1024)}, u32[]{:S(2)}) copy-start(f32[768]{0:T(1024)} %param.16) | copy-start | bytes 9220
  2.2 0.7 copy-start.6
  2.9 0.7 copy-start.7
  3.6 0.7 copy-start.8
  4.2 0.7 copy-start.9
  4.9 0.7 copy-start.10
  115.9 3.0 %copy-start.4 = (f32[768]{0:T(1024)}, f32[768]{0:T(1024)S(1)}, u32[]{:S(2)}) copy-start(f32[768]{0:T(1024)S(1)} %get-tuple-element.85) | copy-start | bytes 9220
  119.5 1.8 %copy-start = (bf16[256,768]{1,0:T(8,128)(2,1)S(1)}, bf16[256,768]{1,0:T(8,128)(2,1)}, u32[]{:S(2)}) copy-start(bf16[256,768]{1,0:T(8,128)(2,1)} %get-tuple-element.79) | copy-start | bytes 1179652
  121.3 1.1 copy-start.3
  122.4 1.1 copy-start.2
  123.4 1.1 copy-start.1

commit v2 on v1

--- a/solution.py
+++ b/solution.py
@@ -824,12 +824,12 @@
             barrier, inc=1, device_id=(f, lax.rem(t + step, tp)), device_id_type=MESH
         ),
     )
-    w_all[0, f] = jnp.concatenate([wq_ref[...], wo_ref[...]], axis=1)
+    w_all[0, f] = jnp.concatenate([wq_ref[...], wo_ref[...].T], axis=1)
     w_all[1, f] = wu_ref[...]
     w_all[2, f] = wd_ref[...]
     c_all[t] = c_ref[...]
     own = x_ref[...].astype(f32)
-    normed, inverse, shifted = layer_norm(own, gain_ref[...], shift_ref[...])
+    normed, inverse, shifted = layer_norm(own, gain_ref[...][None], shift_ref[...][None])
     h_all[t] = shifted.astype(bf16)
     normed_ref[...] = normed
     inverse_ref[...] = inverse
@@ -974,7 +974,7 @@
         weight = w_all[0].reshape(model, model)
         part_of = pl.ds(s * block, block)
         qkv_ref[part_of] = (
-            jnp.dot(h_all[s], weight[:, :wide], preferred_element_type=f32) + bq_ref[...]
+            jnp.dot(h_all[s], weight[:, :wide], preferred_element_type=f32) + bq_ref[...][None]
         )
         return carry
 
@@ -1157,7 +1157,7 @@
         spots = pl.ds(s * block, block)
         up = w_all[1].reshape(model, hidden)
         down = w_all[2].reshape(model, hidden)
-        a = jnp.dot(h_all[s], up, preferred_element_type=f32) + bu_ref[...]
+        a = jnp.dot(h_all[s], up, preferred_element_type=f32) + bu_ref[...][None]
         bell = 0.5 * (1.0 + error_function(a * 0.7071067811865476))
         gelu_ref[spots] = (a * bell).astype(bf16)
         slope = bell + a * jnp.exp(-0.5 * a * a) * 0.3989422804014327
@@ -1276,7 +1276,7 @@
     each(1, fsdp, lambda step: v_copy(step, f).start())
     rows_all[f] = rows[...]
     normed = normed_ref[...]
-    scaled = d_out[...] * gain_ref[...]
+    scaled = d_out[...] * gain_ref[...][None]
     dx_out[...] = (
         c_ref[...].astype(f32)
         + inverse_ref[...]
@@ -1303,7 +1303,9 @@
     each(1, tp, lambda step: u_copy(step, t).start())
     each(2, lines, lambda step: join(2, step))
     gathered(1)
-    y_out[...] = (x_ref[...].astype(f32) + d_out[...] + ob_ref[...] + db_ref[...]).astype(bf16)
+    y_out[...] = (
+        x_ref[...].astype(f32) + d_out[...] + ob_ref[...][None] + db_ref[...][None]
+    ).astype(bf16)
     each(1, tp, lambda step: u_copy(step, lax.rem(t + tp - step, tp)).wait_recv())
     whole = shared[0]
     for step in range(1, tp):
@@ -1428,6 +1430,64 @@
     )(x, c, seg, gain, shift, ob, db, bq, bu, wq, wo, wu, wd)
 
 
+def deliver_kernel(y, dx, gq, go, gu, gd, v, *refs):
+    outs, (turned, sums, sems) = refs[:12], refs[12:]
+    pairs = (
+        (v, sums),
+        (go, turned),
+        (y, outs[0]),
+        (dx, outs[1]),
+        (gq, outs[4]),
+        (gu, outs[8]),
+        (gd, outs[10]),
+    )
+    copies = [
+        pltpu.make_async_copy(source, target, sems.at[i])
+        for i, (source, target) in enumerate(pairs)
+    ]
+    for copy in copies:
+        copy.start()
+    copies[0].wait()
+    for place_of, row in ((2, 0), (3, 1), (5, 8), (7, 2), (9, 9), (11, 2)):
+        outs[place_of][...] = sums[row][: outs[place_of].shape[0]]
+    copies[1].wait()
+    outs[6][...] = turned[...].T
+    for copy in copies[2:]:
+        copy.wait()
+
+
+def deliver(y, dx, gq, go, gu, gd, v):
+    f32 = jnp.float32
+    vmem = pl.BlockSpec(memory_space=pltpu.VMEM)
+    line = jax.ShapeDtypeStruct((y.shape[1],), f32)
+    return pl.pallas_call(
+        deliver_kernel,
+        out_shape=(
+            jax.ShapeDtypeStruct(y.shape, y.dtype),
+            jax.ShapeDtypeStruct(dx.shape, dx.dtype),
+            line,
+            line,
+            jax.ShapeDtypeStruct(gq.shape, f32),
+            jax.ShapeDtypeStruct((gq.shape[1],), f32),
+            jax.ShapeDtypeStruct((go.shape[1], go.shape[0]), f32),
+            line,
+            jax.ShapeDtypeStruct(gu.shape, f32),
+            jax.ShapeDtypeStruct((gu.shape[1],), f32),
+            jax.ShapeDtypeStruct(gd.shape, f32),
+            line,
+        ),
+        in_specs=[pl.BlockSpec(memory_space=pl.ANY)] * 7,
+        out_specs=(vmem,) * 12,
+        scratch_shapes=[
+            pltpu.VMEM(go.shape, f32),
+            pltpu.VMEM(v.shape, f32),
+            pltpu.SemaphoreType.DMA((7,)),
+        ],
+        compiler_params=pltpu.CompilerParams(vmem_limit_bytes=60 * 1024 * 1024),
+        name="deliver",
+    )(y, dx, gq, go, gu, gd, v)
+
+
 def fused_body(
     layer_input,
     out_cotangent,
@@ -1447,31 +1507,20 @@
         layer_input,
         out_cotangent,
         segments,
-        norm_gain[None],
-        norm_bias[None],
-        out_bias[None],
-        down_bias[None],
-        qkv_bias[None],
-        up_bias[None],
+        norm_gain,
+        norm_bias,
+        out_bias,
+        down_bias,
+        qkv_bias,
+        up_bias,
         qkv_weight,
-        out_weight.T,
+        out_weight,
         up_weight,
         down_weight.T,
     )
-    return (
-        y,
-        dx,
-        sums[0],
-        sums[1],
-        qkv_grad,
-        sums[8, : qkv_bias.shape[0]],
-        out_grad.T,
-        sums[2],
-        up_grad,
-        sums[9, : up_bias.shape[0]],
-        down_grad.T,
-        sums[2],
-    )
+    outs = list(deliver(y, dx, qkv_grad, out_grad, up_grad, down_grad, sums))
+    outs[10] = outs[10].T
+    return tuple(outs)
 
 
 def body(*args):

time: 126 us -> 112 us (0.89)
  local copies, waits for them, and re-layouts: 16.3 us -> 0 us
  Pallas kernels: 108 us -> 111 us
    unnamed x30 -> x0, local copies, waits for them, and re-layouts: 10 us -> none
    broadcast_in_dim x6 -> x0, local copies, waits for them, and re-layouts: 3.48 us -> none  [the longest x1 0.58 us: fused_body(): norm_gain[None]]
    slice x2 -> x0, local copies, waits for them, and re-layouts: 2.82 us -> none  [the longest x1 1.48 us: fused_body(): sums[9, :up_bias.shape[0]]]
    pallas_call x0 -> x1, Pallas kernels: none -> 2.71 us  [deliver(): pl.pallas_call(deliver_kernel, out_shape=(jax.ShapeDtypeStruct(y.shape, y...]
where the time goes in v2:
time: 112 us
  Pallas kernels  111 us (99%)
    pallas_call x1, Pallas kernels, layer_call(): pl.pallas_call(functools.partial(layer_kernel, fsdp, tp, heads), out_shap...  108 us
    pallas_call x1, Pallas kernels, deliver(): pl.pallas_call(deliver_kernel, out_shape=(jax.ShapeDtypeStruct(y.shape, y...  2.71 us

profile of v2, /device:TPU:0, one launch (start us, length us, event | category | flops | bytes accessed | tf_op | source)
XLA Modules:
  0.0 111.8 jit_solution(17695574179893962384)
XLA Ops:
  0.6 108.2 %layer.1 = (bf16[256,768]{1,0:T(8,128)(2,1)}, bf16[256,768]{1,0:T(8,128)(2,1)}, f32[96,576]{1,0:T(8,128)}, f32[96,192]{1,0:T(8,128)}, f32[96,768]{1,0:T(8,128)}, /*index=5*/f32[96,768]{1,0:T(8,128)}, f32[16,768]{1,0:T(8,128)}) custom-call(bf16[256,768]{1,0:T(8,128)(2,1)} %x_ref.1, bf16[256,768]{1,0:T(8,128)(2,1)} %c_ref.1, s32[1,1024]{1,0:T(1,128)} %seg_ref.1, ...), custom_call_target="tpu_custom_call" | custom-call | tf_op jit(solution)/shard_map/layer/pallas_call | solution.py:1370
  108.9 2.7 %deliver.1 = (bf16[256,768]{1,0:T(8,128)(2,1)}, bf16[256,768]{1,0:T(8,128)(2,1)}, f32[768]{0:T(1024)}, f32[768]{0:T(1024)}, f32[96,576]{1,0:T(8,128)}, /*index=5...) custom-call(bf16[256,768]{1,0:T(8,128)(2,1)} %get-tuple-element.31.y, ...), custom_call_target="tpu_custom_call" | custom-call | tf_op jit(solution)/shard_map/deliver/pallas_call | solution.py:1463

commit v3 on v2

--- a/solution.py
+++ b/solution.py
@@ -768,6 +768,7 @@
     shared,
     up_send,
     down_send,
+    far_send,
     z_recv,
     y_send,
     y_recv,
@@ -848,6 +849,22 @@
     def z_down(i, origin):
         return z_copy(i, origin, down_send, line - 1)
 
+    last_line = lines - 1
+    direct = lines > 2
+
+    def far(i):
+        view = w_all.at[i, f]
+        return remote(
+            view,
+            view,
+            far_send.at[i],
+            z_recv.at[i, line],
+            (2 * (last_line - line) + pair, t),
+        )
+
+    def at_end():
+        return (line == 0) | (line == last_line)
+
     def y_copy(i, origin, side_of):
         view = w_all.at[i, 2 * origin + side_of]
         return remote(view, view, y_send.at[i, origin], y_recv.at[i, origin], (partner, t))
@@ -862,6 +879,11 @@
             z_down(i, line).start()
 
         y_copy(i, line, pair).start()
+        if direct:
+
+            @pl.when(at_end())
+            def _():
+                far(i).start()
 
     def relay(r):
         i = lax.div(r, lines - 1)
@@ -873,7 +895,7 @@
         def _():
             z_up(i, below).wait_recv()
 
-            @pl.when(line + 1 < lines)
+            @pl.when((line + 1 < lines) & (not direct or (line + 1 - below < last_line)))
             def _():
                 z_up(i, below).start()
 
@@ -883,7 +905,7 @@
         def _():
             z_down(i, above).wait_recv()
 
-            @pl.when(line > 0)
+            @pl.when((line > 0) & (not direct or (above - line + 1 < last_line)))
             def _():
                 z_down(i, above).start()
 
@@ -1258,10 +1280,6 @@
     rows[...] = jnp.zeros_like(rows)
     rows[0:1] = jnp.sum(d_out[...] * normed_ref[...], axis=0, keepdims=True)
     rows[1:2] = jnp.sum(d_out[...], axis=0, keepdims=True)
-    each(1, fsdp, lambda step: e_copy(step, lax.rem(f + fsdp - step, fsdp)).wait_recv())
-    early_all[f] = early[...]
-    total = lax.fori_loop(1, fsdp, lambda step, value: value + early_all[step], early_all[0])
-    v_out[8:16] = total
     rows[2:3] = early[2:3]
 
     def v_copy(step, place_of):
@@ -1286,7 +1304,16 @@
             - normed * jnp.mean(scaled * normed, axis=-1, keepdims=True)
         )
     ).astype(bf16)
-    join(2, 1)
+    each(1, lines - 1, lambda step: join(2, step))
+    gathered(1)
+    y_out[...] = (
+        x_ref[...].astype(f32) + d_out[...] + ob_ref[...][None] + db_ref[...][None]
+    ).astype(bf16)
+    each(lines - 1, lines, lambda step: join(2, step))
+    each(1, fsdp, lambda step: e_copy(step, lax.rem(f + fsdp - step, fsdp)).wait_recv())
+    early_all[f] = early[...]
+    total = lax.fori_loop(1, fsdp, lambda step, value: value + early_all[step], early_all[0])
+    v_out[8:16] = total
     each(1, fsdp, lambda step: v_copy(step, lax.rem(f + fsdp - step, fsdp)).wait_recv())
     shared[t] = lax.fori_loop(1, fsdp, lambda step, value: value + rows_all[step], rows_all[0])
 
@@ -1301,42 +1328,45 @@
         )
 
     each(1, tp, lambda step: u_copy(step, t).start())
-    each(2, lines, lambda step: join(2, step))
-    gathered(1)
-    y_out[...] = (
-        x_ref[...].astype(f32) + d_out[...] + ob_ref[...][None] + db_ref[...][None]
-    ).astype(bf16)
+    def collected(i):
+        across(i, 0).wait_recv()
+        value = g_all[i, f].astype(f32) + halves[i, 0].astype(f32)
+
+        def one(step, value):
+            along(i, step).wait_recv()
+            return value + lands[i, step].astype(f32)
+
+        return lax.fori_loop(1, lines, one, value)
+
+    value = collected(0)
+    gq_out[...] = value[:, :wide]
+    go_out[...] = value[:, wide:]
+    gu_out[...] = collected(1)
+    gd_out[...] = collected(2)
+
     each(1, tp, lambda step: u_copy(step, lax.rem(t + tp - step, tp)).wait_recv())
     whole = shared[0]
     for step in range(1, tp):
         whole = whole + shared[step]
     v_out[0:8] = whole
 
-    def collected(i):
-        across(i, 0).wait_recv()
-        value = g_all[i, f].astype(f32) + halves[i, 0].astype(f32)
-
-        def one(step, value):
-            along(i, step).wait_recv()
-            return value + lands[i, step].astype(f32)
-
-        return lax.fori_loop(1, lines, one, value)
-
-    value = collected(0)
-    gq_out[...] = value[:, :wide]
-    go_out[...] = value[:, wide:]
-    gu_out[...] = collected(1)
-    gd_out[...] = collected(2)
-
     for i in range(3):
 
         @pl.when(line + 1 < lines)
         def _():
-            each(0, line + 1, lambda origin: z_up(i, origin).wait_send())
+            first = jnp.maximum(0, line + 2 - last_line) if direct else 0
+            each(first, line + 1, lambda origin: z_up(i, origin).wait_send())
 
         @pl.when(line > 0)
         def _():
-            each(line, lines, lambda origin: z_down(i, origin).wait_send())
+            end = jnp.minimum(lines, line + last_line - 1) if direct else lines
+            each(line, end, lambda origin: z_down(i, origin).wait_send())
+
+        if direct:
+
+            @pl.when(at_end())
+            def _():
+                far(i).wait_send()
 
         each(0, lines, lambda origin: y_copy(i, origin, pair).wait_send())
         each(0, lines, lambda step: across(i, step).wait_send())
@@ -1417,7 +1447,9 @@
             buf((fsdp, 8, model), f32),
             buf((tp, 8, model), f32),
         ]
-        + [dma((3, lines))] * 5
+        + [dma((3, lines))] * 2
+        + [dma((3,))]
+        + [dma((3, lines))] * 3
         + [dma((2, sides))] * 4
         + [dma((3, lines))] * 4
         + [dma((2, sides))] * 4

time: 112 us -> 120 us (1.071)
  Pallas kernels: 111 us -> 118 us
    pallas_call x1, Pallas kernels: 108 us -> 115 us  [layer_call(): pl.pallas_call(functools.partial(layer_kernel, fsdp, tp, heads), out_shap...]
where the time goes in v3:
time: 120 us; the launch traced here: 119 us
  Pallas kernels  118 us (98%)
    pallas_call x1, Pallas kernels, layer_call(): pl.pallas_call(functools.partial(layer_kernel, fsdp, tp, heads), out_shap...  115 us
    pallas_call x1, Pallas kernels, deliver(): pl.pallas_call(deliver_kernel, out_shape=(jax.ShapeDtypeStruct(y.shape, y...  2.71 us

profile of v3, /device:TPU:0, one launch (start us, length us, event | category | flops | bytes accessed | tf_op | source)
XLA Modules:
  0.0 118.9 jit_solution(4669324038755380494)
XLA Ops:
  0.6 115.4 %layer.1 = (bf16[256,768]{1,0:T(8,128)(2,1)}, bf16[256,768]{1,0:T(8,128)(2,1)}, f32[96,576]{1,0:T(8,128)}, f32[96,192]{1,0:T(8,128)}, f32[96,768]{1,0:T(8,128)}, /*index=5*/f32[96,768]{1,0:T(8,128)}, f32[16,768]{1,0:T(8,128)}) custom-call(bf16[256,768]{1,0:T(8,128)(2,1)} %x_ref.1, bf16[256,768]{1,0:T(8,128)(2,1)} %c_ref.1, s32[1,1024]{1,0:T(1,128)} %seg_ref.1, ...), custom_call_target="tpu_custom_call" | custom-call | tf_op jit(solution)/shard_map/layer/pallas_call | solution.py:1400
  116.0 2.7 %deliver.1 = (bf16[256,768]{1,0:T(8,128)(2,1)}, bf16[256,768]{1,0:T(8,128)(2,1)}, f32[768]{0:T(1024)}, f32[768]{0:T(1024)}, f32[96,576]{1,0:T(8,128)}, /*index=5...) custom-call(bf16[256,768]{1,0:T(8,128)(2,1)} %get-tuple-element.31.y, ...), custom_call_target="tpu_custom_call" | custom-call | tf_op jit(solution)/shard_map/deliver/pallas_call | solution.py:1495
